TPU v7x, 32 devices: a whole 2x2x4 slice. The times are simulated.
32 devices in a mesh: fsdp: 4 (over y, x), ctx: 2 (over core), tp: 4 (over z).
Axes of the slice: x: 2, y: 2, z: 4, core: 2. Of those that a mesh axis runs over, the one named last changes fastest.
Arguments:
- tokens: bfloat16 [4, 2048, 2048], P('fsdp', 'ctx'), may hold values from -6 to 6
- cotangent: bfloat16 [4, 2048, 2048], P('fsdp', 'ctx'), may hold values from -6 to 6
- piece_starts: int32 [4, 3], P('fsdp'), may hold values from 0 to 1790, as said below
- attn_gain: bfloat16 [2048], P(('fsdp', 'ctx')), may hold values from 0.5 to 1.5
- query_down: bfloat16 [2048, 1024], P(('fsdp', 'ctx')), may hold values from -0.125 to 0.125
- query_gain: bfloat16 [1024], P(('fsdp', 'ctx')), may hold values from 0.5 to 1.5
- query_up: bfloat16 [1024, 4096], P(('fsdp', 'ctx'), 'tp'), may hold values from -0.1875 to 0.1875
- key_proj: bfloat16 [2048, 256], P(('fsdp', 'ctx')), may hold values from -0.125 to 0.125
- value_proj: bfloat16 [2048, 256], P(('fsdp', 'ctx')), may hold values from -0.125 to 0.125
- out_proj: bfloat16 [4096, 2048], P('tp', ('fsdp', 'ctx')), may hold values from -1 to 1
- ffn_gain: bfloat16 [2048], P(('fsdp', 'ctx')), may hold values from 0.5 to 1.5
- gate_proj: bfloat16 [2048, 5632], P(('fsdp', 'ctx'), 'tp'), may hold values from -0.125 to 0.125
- up_proj: bfloat16 [2048, 5632], P(('fsdp', 'ctx'), 'tp'), may hold values from -0.125 to 0.125
- down_proj: bfloat16 [5632, 2048], P('tp', ('fsdp', 'ctx')), may hold values from -0.078125 to 0.078125
Outputs:
- layer_out: bfloat16 [4, 2048, 2048], P('fsdp', 'ctx')
- tokens_grad: bfloat16 [4, 2048, 2048], P('fsdp', 'ctx')
- attn_gain_grad: float32 [2048], P(('fsdp', 'ctx'))
- query_down_grad: float32 [2048, 1024], P(('fsdp', 'ctx'))
- query_gain_grad: float32 [1024], P(('fsdp', 'ctx'))
- query_up_grad: float32 [1024, 4096], P(('fsdp', 'ctx'), 'tp')
- key_proj_grad: float32 [2048, 256], P(('fsdp', 'ctx'))
- value_proj_grad: float32 [2048, 256], P(('fsdp', 'ctx'))
- out_proj_grad: float32 [4096, 2048], P('tp', ('fsdp', 'ctx'))
- ffn_gain_grad: float32 [2048], P(('fsdp', 'ctx'))
- gate_proj_grad: float32 [2048, 5632], P(('fsdp', 'ctx'), 'tp')
- up_proj_grad: float32 [2048, 5632], P(('fsdp', 'ctx'), 'tp')
- down_proj_grad: float32 [5632, 2048], P('tp', ('fsdp', 'ctx'))
Inputs may be any that keep to these rules, and one draw needn't show every extreme that they name: `piece_starts`: in each sequence piece k starts at or after k * (682) and ends by (k + 1) * 682, so pieces never intersect and starts rise.
All inputs are finite; a program needn't handle non-finite values.
Results may differ from a plain program's by a relative error of at most 0.024.
Values may be sent and summed in bfloat16 or wider, within the bound.
No kernel may reach another device: no remote copies, remote signals or barrier semaphores. Data moves between devices by JAX's collectives and lax.ppermute only.
A program may use at most 256 MiB of HBM per device.

v0:
```python
import jax
import jax.numpy as jnp
from jax import lax
from jax.sharding import PartitionSpec as P

PIECE = 256
norm_eps = 1e-05
masked_score = -1e30


def rope_tables(positions, width):
    half_width = width // 2
    freqs = jnp.exp(-jnp.log(10000.0) * jnp.arange(half_width).astype(jnp.float32) * 2.0 / width)
    angles = positions.astype(jnp.float32)[:, None] * freqs[None, :]
    return (jnp.cos(angles), jnp.sin(angles))


def rotate(vectors, cosine, sine):
    half_width = vectors.shape[-1] // 2
    first, second = (vectors[..., :half_width], vectors[..., half_width:])
    return jnp.concatenate(
        [first * cosine - second * sine, second * cosine + first * sine], axis=-1
    )


def unrotate(vectors, cosine, sine):
    half_width = vectors.shape[-1] // 2
    first, second = (vectors[..., :half_width], vectors[..., half_width:])
    return jnp.concatenate(
        [first * cosine + second * sine, second * cosine - first * sine], axis=-1
    )


def piece_ids(positions, starts):
    inside = (positions[:, None] >= starts[None, :]) & (
        positions[:, None] < starts[None, :] + PIECE
    )
    numbers = jnp.arange(1, starts.shape[0] + 1)
    return jnp.sum(jnp.where(inside, numbers[None, :], 0), axis=1) - 1


def normalize(values, norm_weight):
    inverse = lax.rsqrt(jnp.mean(values * values, axis=-1, keepdims=True) + norm_eps)
    return (values * inverse * norm_weight.astype(jnp.float32), inverse)


def norm_back(values, inverse, norm_weight, upstream):
    weighted = upstream * norm_weight.astype(jnp.float32)
    weight_grad = jnp.sum(upstream * values * inverse, axis=0)
    value_grad = inverse * weighted - values * inverse * inverse * inverse * jnp.mean(
        weighted * values, axis=-1, keepdims=True
    )
    return (value_grad, weight_grad)


def matmul(left, right):
    return jnp.dot(left, right, preferred_element_type=jnp.float32)


def matmul_tn(left, right):
    return lax.dot_general(
        left, right, (((0,), (0,)), ((), ())), preferred_element_type=jnp.float32
    )


def matmul_nt(left, right):
    return lax.dot_general(
        left, right, (((1,), (1,)), ((), ())), preferred_element_type=jnp.float32
    )


def shards(
    tokens,
    cotangent,
    piece_starts,
    attn_gain,
    query_down,
    query_gain,
    query_up,
    key_proj,
    value_proj,
    out_proj,
    ffn_gain,
    gate_proj,
    up_proj,
    down_proj,
):
    seq_count, half_len, width = tokens.shape
    row_count = seq_count * half_len
    full_len = half_len * lax.axis_size("ctx")
    (
        full_attn_gain,
        full_query_down,
        full_query_gain,
        full_query_up,
        full_key_proj,
        full_value_proj,
        full_out_proj,
        full_ffn_gain,
        full_gate_proj,
        full_up_proj,
        full_down_proj,
    ) = (
        lax.all_gather(attn_gain, ("fsdp", "ctx"), axis=0, tiled=True),
        lax.all_gather(query_down, ("fsdp", "ctx"), axis=0, tiled=True),
        lax.all_gather(query_gain, ("fsdp", "ctx"), axis=0, tiled=True),
        lax.all_gather(query_up, ("fsdp", "ctx"), axis=0, tiled=True),
        lax.all_gather(key_proj, ("fsdp", "ctx"), axis=0, tiled=True),
        lax.all_gather(value_proj, ("fsdp", "ctx"), axis=0, tiled=True),
        lax.all_gather(out_proj, ("fsdp", "ctx"), axis=1, tiled=True),
        lax.all_gather(ffn_gain, ("fsdp", "ctx"), axis=0, tiled=True),
        lax.all_gather(gate_proj, ("fsdp", "ctx"), axis=0, tiled=True),
        lax.all_gather(up_proj, ("fsdp", "ctx"), axis=0, tiled=True),
        lax.all_gather(down_proj, ("fsdp", "ctx"), axis=1, tiled=True),
    )
    head_dim = full_key_proj.shape[1]
    local_heads = full_query_up.shape[1] // head_dim
    score_scale = head_dim ** (-0.5)
    row_start_ctx = lax.axis_index("ctx") * half_len
    positions = row_start_ctx + jnp.arange(half_len)
    key_positions = jnp.arange(full_len)
    cosine, sine = rope_tables(positions, head_dim)
    key_labels = jax.vmap(lambda starts: piece_ids(key_positions, starts))(piece_starts)
    query_labels = lax.dynamic_slice_in_dim(key_labels, row_start_ctx, half_len, 1)
    rows_in = tokens.reshape(row_count, width).astype(jnp.float32)
    normed_one, inverse_one = normalize(rows_in, full_attn_gain)
    normed_one = normed_one.astype(jnp.bfloat16)
    latent = matmul(normed_one, full_query_down)
    latent_normed, inverse_latent = normalize(latent, full_query_gain)
    latent_normed = latent_normed.astype(jnp.bfloat16)
    query_lin = matmul(latent_normed, full_query_up).reshape(
        seq_count, half_len, local_heads, head_dim
    )
    queries = rotate(query_lin, cosine[None, :, None, :], sine[None, :, None, :]).astype(
        jnp.bfloat16
    )
    key_lin = matmul(normed_one, full_key_proj).reshape(seq_count, half_len, head_dim)
    key_local = rotate(key_lin, cosine[None], sine[None]).astype(jnp.bfloat16)
    value_local = (
        matmul(normed_one, full_value_proj)
        .astype(jnp.bfloat16)
        .reshape(seq_count, half_len, head_dim)
    )
    kv_local = jnp.concatenate([key_local, value_local], axis=-1)
    kv_full = lax.all_gather(kv_local, "ctx", axis=1, tiled=True)
    block_rows = min(512, half_len)
    per_seq = half_len // block_rows
    block_total = seq_count * per_seq

    def block_scores(block_index):
        seq_index = block_index // per_seq
        row_start = block_index % per_seq * block_rows
        query_block = lax.dynamic_slice(
            queries, (seq_index, row_start, 0, 0), (1, block_rows, local_heads, head_dim)
        )[0]
        kv_seq = lax.dynamic_index_in_dim(kv_full, seq_index, 0, keepdims=False)
        key_rows = kv_seq[:, :head_dim]
        value_rows = kv_seq[:, head_dim:]
        scores = (
            jnp.einsum("qhd,kd->hqk", query_block, key_rows, preferred_element_type=jnp.float32)
            * score_scale
        )
        query_pos = lax.dynamic_slice_in_dim(positions, row_start, block_rows, 0)
        query_lab = lax.dynamic_slice(query_labels, (seq_index, row_start), (1, block_rows))[0]
        key_lab = lax.dynamic_index_in_dim(key_labels, seq_index, 0, keepdims=False)
        allowed = (key_positions[None, :] <= query_pos[:, None]) | (
            query_lab[:, None] == key_lab[None, :]
        ) & (query_lab[:, None] >= 0)
        scores = jnp.where(allowed[None], scores, masked_score)
        return (seq_index, row_start, query_block, key_rows, value_rows, scores)

    def attend(block_index):
        seq_index, row_start, query_block, key_rows, value_rows, scores = block_scores(block_index)
        top_score = jnp.max(scores, axis=-1, keepdims=True)
        expo = jnp.exp(scores - top_score)
        total = jnp.sum(expo, axis=-1, keepdims=True)
        attn_probs = (expo / total).astype(jnp.bfloat16)
        block_out = jnp.einsum(
            "hqk,kd->qhd", attn_probs, value_rows, preferred_element_type=jnp.float32
        )
        return (block_out, (top_score + jnp.log(total))[..., 0])

    blocks_out, log_totals = lax.map(attend, jnp.arange(block_total))
    attended = blocks_out.reshape(row_count, local_heads * head_dim).astype(jnp.bfloat16)
    attn_terms = matmul(attended, full_out_proj)
    hidden_part = rows_in + lax.psum(attn_terms.astype(jnp.bfloat16), "tp").astype(jnp.float32)
    normed_two, inverse_two = normalize(hidden_part, full_ffn_gain)
    normed_two = normed_two.astype(jnp.bfloat16)
    gate_vals = matmul(normed_two, full_gate_proj)
    up_vals = matmul(normed_two, full_up_proj)
    sigmoid_gate = jax.nn.sigmoid(gate_vals)
    silu_gate = gate_vals * sigmoid_gate
    activ = (silu_gate * up_vals).astype(jnp.bfloat16)
    ffn_terms = matmul(activ, full_down_proj)
    layer_rows = (
        hidden_part + lax.psum(ffn_terms.astype(jnp.bfloat16), "tp").astype(jnp.float32)
    ).astype(jnp.bfloat16)
    layer_out = layer_rows.reshape(tokens.shape)
    upstream = cotangent.reshape(row_count, width)
    d_activ = matmul_nt(upstream, full_down_proj)
    down_grad = matmul_tn(activ, upstream)
    d_gate = (d_activ * up_vals * sigmoid_gate * (1.0 + gate_vals * (1.0 - sigmoid_gate))).astype(
        jnp.bfloat16
    )
    d_up = (d_activ * silu_gate).astype(jnp.bfloat16)
    gate_grad = matmul_tn(normed_two, d_gate)
    up_grad = matmul_tn(normed_two, d_up)
    d_norm_terms = matmul_nt(d_gate, full_gate_proj) + matmul_nt(d_up, full_up_proj)
    d_normed_two = lax.psum(d_norm_terms.astype(jnp.bfloat16), "tp").astype(jnp.float32)
    d_hidden_norm, ffn_gain_grad = norm_back(hidden_part, inverse_two, full_ffn_gain, d_normed_two)
    d_hidden = upstream.astype(jnp.float32) + d_hidden_norm
    d_mixed = d_hidden.astype(jnp.bfloat16)
    out_grad = matmul_tn(attended, d_mixed)
    d_attended = (
        matmul_nt(d_mixed, full_out_proj)
        .astype(jnp.bfloat16)
        .reshape(seq_count, half_len, local_heads, head_dim)
    )

    def attend_back(kv_grad, block_index):
        seq_index, row_start, query_block, key_rows, value_rows, scores = block_scores(block_index)
        attn_probs = jnp.exp(scores - log_totals[block_index][..., None])
        d_out_block = lax.dynamic_slice(
            d_attended, (seq_index, row_start, 0, 0), (1, block_rows, local_heads, head_dim)
        )[0]
        d_probs = jnp.einsum(
            "qhd,kd->hqk", d_out_block, value_rows, preferred_element_type=jnp.float32
        )
        inner = jnp.sum(attn_probs * d_probs, axis=-1, keepdims=True)
        d_scores = (attn_probs * (d_probs - inner)).astype(jnp.bfloat16)
        d_query = (
            jnp.einsum("hqk,kd->qhd", d_scores, key_rows, preferred_element_type=jnp.float32)
            * score_scale
        )
        d_key_rows = (
            jnp.einsum("hqk,qhd->kd", d_scores, query_block, preferred_element_type=jnp.float32)
            * score_scale
        )
        d_value_rows = jnp.einsum(
            "hqk,qhd->kd",
            attn_probs.astype(jnp.bfloat16),
            d_out_block,
            preferred_element_type=jnp.float32,
        )
        kv_grad = kv_grad.at[seq_index].add(jnp.concatenate([d_key_rows, d_value_rows], axis=-1))
        return (kv_grad, d_query)

    kv_grad_full, d_query_blocks = lax.scan(
        attend_back,
        jnp.zeros((seq_count, full_len, 2 * head_dim), jnp.float32),
        jnp.arange(block_total),
    )
    d_queries = d_query_blocks.reshape(seq_count, half_len, local_heads, head_dim)
    d_query_lin = (
        unrotate(d_queries, cosine[None, :, None, :], sine[None, :, None, :])
        .reshape(row_count, local_heads * head_dim)
        .astype(jnp.bfloat16)
    )
    query_up_grad = matmul_tn(latent_normed, d_query_lin)
    d_latent_part = matmul_nt(d_query_lin, full_query_up)
    kv_grad_local = lax.psum_scatter(
        kv_grad_full.astype(jnp.bfloat16), "ctx", scatter_dimension=1, tiled=True
    )
    d_latent_normed, kv_grad_sum = (
        lax.psum(d_latent_part.astype(jnp.bfloat16), "tp").astype(jnp.float32),
        lax.psum(kv_grad_local, "tp").astype(jnp.float32),
    )
    d_key_lin = (
        unrotate(kv_grad_sum[..., :head_dim], cosine[None], sine[None])
        .reshape(row_count, head_dim)
        .astype(jnp.bfloat16)
    )
    d_value_lin = kv_grad_sum[..., head_dim:].reshape(row_count, head_dim).astype(jnp.bfloat16)
    d_latent, query_gain_grad = norm_back(latent, inverse_latent, full_query_gain, d_latent_normed)
    d_latent = d_latent.astype(jnp.bfloat16)
    query_down_grad = matmul_tn(normed_one, d_latent)
    key_grad = matmul_tn(normed_one, d_key_lin)
    value_grad = matmul_tn(normed_one, d_value_lin)
    d_normed_one = (
        matmul_nt(d_latent, full_query_down)
        + matmul_nt(d_key_lin, full_key_proj)
        + matmul_nt(d_value_lin, full_value_proj)
    )
    d_rows_norm, attn_gain_grad = norm_back(rows_in, inverse_one, full_attn_gain, d_normed_one)
    tokens_grad = (d_hidden + d_rows_norm).astype(jnp.bfloat16).reshape(tokens.shape)
    grad_shards = (
        lax.psum_scatter(
            attn_gain_grad.astype(jnp.bfloat16), ("fsdp", "ctx"), scatter_dimension=0, tiled=True
        ).astype(jnp.float32),
        lax.psum_scatter(
            query_down_grad.astype(jnp.bfloat16), ("fsdp", "ctx"), scatter_dimension=0, tiled=True
        ).astype(jnp.float32),
        lax.psum_scatter(
            query_gain_grad.astype(jnp.bfloat16), ("fsdp", "ctx"), scatter_dimension=0, tiled=True
        ).astype(jnp.float32),
        lax.psum_scatter(
            query_up_grad.astype(jnp.bfloat16), ("fsdp", "ctx"), scatter_dimension=0, tiled=True
        ).astype(jnp.float32),
        lax.psum_scatter(
            key_grad.astype(jnp.bfloat16), ("fsdp", "ctx"), scatter_dimension=0, tiled=True
        ).astype(jnp.float32),
        lax.psum_scatter(
            value_grad.astype(jnp.bfloat16), ("fsdp", "ctx"), scatter_dimension=0, tiled=True
        ).astype(jnp.float32),
        lax.psum_scatter(
            out_grad.astype(jnp.bfloat16), ("fsdp", "ctx"), scatter_dimension=1, tiled=True
        ).astype(jnp.float32),
        lax.psum_scatter(
            ffn_gain_grad.astype(jnp.bfloat16), ("fsdp", "ctx"), scatter_dimension=0, tiled=True
        ).astype(jnp.float32),
        lax.psum_scatter(
            gate_grad.astype(jnp.bfloat16), ("fsdp", "ctx"), scatter_dimension=0, tiled=True
        ).astype(jnp.float32),
        lax.psum_scatter(
            up_grad.astype(jnp.bfloat16), ("fsdp", "ctx"), scatter_dimension=0, tiled=True
        ).astype(jnp.float32),
        lax.psum_scatter(
            down_grad.astype(jnp.bfloat16), ("fsdp", "ctx"), scatter_dimension=1, tiled=True
        ).astype(jnp.float32),
    )
    return (layer_out, tokens_grad) + tuple(grad_shards)


def solution(mesh):
    return jax.shard_map(
        shards,
        mesh=mesh,
        in_specs=(
            P("fsdp", "ctx", None),
            P("fsdp", "ctx", None),
            P("fsdp", None),
            P(("fsdp", "ctx")),
            P(("fsdp", "ctx"), None),
            P(("fsdp", "ctx")),
            P(("fsdp", "ctx"), "tp"),
            P(("fsdp", "ctx"), None),
            P(("fsdp", "ctx"), None),
            P("tp", ("fsdp", "ctx")),
            P(("fsdp", "ctx")),
            P(("fsdp", "ctx"), "tp"),
            P(("fsdp", "ctx"), "tp"),
            P("tp", ("fsdp", "ctx")),
        ),
        out_specs=(
            P("fsdp", "ctx", None),
            P("fsdp", "ctx", None),
            P(("fsdp", "ctx")),
            P(("fsdp", "ctx"), None),
            P(("fsdp", "ctx")),
            P(("fsdp", "ctx"), "tp"),
            P(("fsdp", "ctx"), None),
            P(("fsdp", "ctx"), None),
            P("tp", ("fsdp", "ctx")),
            P(("fsdp", "ctx")),
            P(("fsdp", "ctx"), "tp"),
            P(("fsdp", "ctx"), "tp"),
            P("tp", ("fsdp", "ctx")),
        ),
        check_vma=False,
    )
```

profile of v0, /device:TPU:0, one launch (start us, length us, event | category | flops | bytes accessed | tf_op | source)
XLA Modules:
  0.0 1569.4 jit_solution(9847680212511088203)
XLA Ops:
  23.0 13.0 all-gather.17.cloned.1.call-done
  42.3 19.0 %all-gather.19.cloned.1.call-done = bf16[2048,256]{1,0:T(8,128)(2,1)} async-done(((bf16[256,256]{1,0:T(8,128)(2,1)}), bf16[2048,256]{1,0:T(8,128)(2,1)}) %all-gather.19.cloned.1.call-update) | async-done | bytes 1048592 | tf_op jit(solution)/shard_map/all_gather | solution.py:109
  82.5 34.1 %all-gather.13.cloned.1.call-done = bf16[2048,1024]{1,0:T(8,128)(2,1)} async-done(((bf16[256,1024]{1,0:T(8,128)(2,1)}), bf16[2048,1024]{1,0:T(8,128)(2,1)}) %all-gather.13.cloned.1.call-update) | async-done | bytes 4194320 | tf_op jit(solution)/shard_map/all_gather | solution.py:105
  126.8 19.4 %all-gather.15.cloned.1.call-done = bf16[1024,1024]{1,0:T(8,128)(2,1)} async-done(((bf16[128,1024]{1,0:T(8,128)(2,1)}), bf16[1024,1024]{1,0:T(8,128)(2,1)}) %all-gather.15.cloned.1.call-update) | async-done | bytes 2097168 | tf_op jit(solution)/shard_map/all_gather | solution.py:107
  164.1 37.7 %while.31 = (s32[]{:T(128)}, bf16[2,512,4,256]{3,1,2,0:T(8,128)(2,1)}, f32[2,4,512]{2,1,0:T(4,128)S(1)}, s32[2]{0:T(128)S(1)}, s32[1024]{0:T(1024)S(1)}, /*index...) while((s32[]{:T(128)}, ...), condition=%wide.region_6.7_spmd.clone, body=%wide.region_3.6_spmd.clone.sunk | while | flops 4349491712 | bytes 59858748 | solution.py:183
  227.4 144.1 %all-reduce.9.cloned.1.call-done = bf16[1024,2048]{1,0:T(8,128)(2,1)} async-done(((bf16[1024,2048]{1,0:T(8,128)(2,1)}), bf16[1024,2048]{1,0:T(8,128)(2,1)}) %all-reduce.9.cloned.1.call-update) | async-done | bytes 4194320 | tf_op jit(solution)/shard_map/psum | solution.py:186
  381.6 33.9 %all-gather.25.cloned.1.call-done = bf16[2048,1408]{1,0:T(8,128)(2,1)} async-done(((bf16[256,1408]{1,0:T(8,128)(2,1)}), bf16[2048,1408]{1,0:T(8,128)(2,1)}) %all-gather.25.cloned.1.call-update) | async-done | bytes 5767184 | tf_op jit(solution)/shard_map/all_gather | solution.py:112
  415.5 11.7 fusion.130
  427.2 33.4 %all-gather.27.cloned.1.call-done = bf16[2048,1408]{1,0:T(8,128)(2,1)} async-done(((bf16[256,1408]{1,0:T(8,128)(2,1)}), bf16[2048,1408]{1,0:T(8,128)(2,1)}) %all-gather.27.cloned.1.call-update) | async-done | bytes 5767184 | tf_op jit(solution)/shard_map/all_gather | solution.py:113
  460.6 11.7 fusion.131
  472.3 34.3 %all-gather.29.cloned.1.call-done = bf16[1408,2048]{1,0:T(8,128)(2,1)} async-done(((bf16[1408,256]{1,0:T(8,128)(2,1)}), bf16[1408,2048]{1,0:T(8,128)(2,1)}) %all-gather.29.cloned.1.call-update) | async-done | bytes 5767184 | tf_op jit(solution)/shard_map/all_gather | solution.py:114
  506.7 15.6 multiply_convert_fusion.1
  542.0 155.1 %all-reduce.11.cloned.1.call-done = bf16[1024,2048]{1,0:T(8,128)(2,1)} async-done(((bf16[1024,2048]{1,0:T(8,128)(2,1)}), bf16[1024,2048]{1,0:T(8,128)(2,1)}) %all-reduce.11.cloned.1.call-update) | async-done | bytes 4194320 | tf_op jit(solution)/shard_map/psum | solution.py:209
  715.0 144.2 %while.32 = (s32[]{:T(128)}, f32[1,2048,512]{1,2,0:T(8,128)}, f32[2,512,4,256]{3,1,0,2:T(8,128)}, s32[2]{0:T(128)S(1)}, s32[1024]{0:T(1024)S(1)}, /*index=5*/s32...) while((s32[]{:T(128)}, f32[1,2048,512]{1,2,0:T(8,128)}, ...), condition=%wide.region_15.16_spmd.clone, body=%wide.region_12.15_spmd.clone.sunk | while | flops 10809767936 | bytes 248594592 | solution.py:248
  730.0 13.1 fusion.193
  743.1 15.9 %fusion.194 = bf16[4,512,2048]{2,1,0:T(8,128)(2,1)} fusion(f32[512,4,2048]{2,0,1:T(8,128)} %get-tuple-element.653, f32[512,4,2048]{2,0,1:T(8,128)} %fusion.190, f32[4,512]{1,0:T(4,128)S(1)} %get-tuple-element.654, f32[4,512]{1,0:T(4,128)S(1)} %dynamic-slice_bitcast_fusion.2, pred[512,2048]{1,0:T(8,128)(4,1)S(1)} %fusion.191), kind=kLoop, calls=%fused_computation.27.clone.1 | loop fusion | flops 25165824 | bytes 43008000 | tf_op jit(solution)/shard_map/while/body/eval_jaxpr/convert_element_type | solution.py:230
  801.2 13.1 fusion.193
  814.3 15.9 %fusion.194 = bf16[4,512,2048]{2,1,0:T(8,128)(2,1)} fusion(f32[512,4,2048]{2,0,1:T(8,128)} %get-tuple-element.653, f32[512,4,2048]{2,0,1:T(8,128)} %fusion.190, f32[4,512]{1,0:T(4,128)S(1)} %get-tuple-element.654, f32[4,512]{1,0:T(4,128)S(1)} %dynamic-slice_bitcast_fusion.2, pred[512,2048]{1,0:T(8,128)(4,1)S(1)} %fusion.191), kind=kLoop, calls=%fused_computation.27.clone.1 | loop fusion | flops 25165824 | bytes 43008000 | tf_op jit(solution)/shard_map/while/body/eval_jaxpr/convert_element_type | solution.py:230
  863.3 11.0 convolution_convert_fusion.3
  893.2 11.0 convolution_convert_fusion.2
  904.3 11.1 convolution_convert_fusion.1
  927.5 14.8 convolution_convert_fusion.4
  942.4 199.2 %all-reduce.13.cloned.1.call-done = (bf16[1024,2048]{1,0:T(8,128)(2,1)}, bf16[1024,1024]{0,1:T(8,128)(2,1)}, bf16[1,1024,512]{1,2,0:T(8,128)(2,1)}) async-done(((bf16[1024,2048]{1,0:T(8,128)(2,1)}, bf16[1024,1024]{0,1:T(8,128)(2,1)}, bf16[1,1024,512]{1,2,0:T(8,128)(2,1)}), (bf16[1024,2048]{1,0:T(8,128)(2,1)}, bf16[1024,1024]{0,1:T(8,128)(2,1)}, ...) | async-done | bytes 7340048 | tf_op jit(solution)/shard_map/psum | solution.py:196
  1170.9 13.9 reduce-scatter.14.cloned.1.call-done
  1186.6 60.5 %reduce-scatter.22.cloned.1.call-done = bf16[256,1408]{1,0:T(8,128)(2,1)} async-done(((bf16[2048,1408]{1,0:T(8,128)(2,1)}), bf16[256,1408]{1,0:T(8,128)(2,1)}) %reduce-scatter.22.cloned.1.call-update) | async-done | bytes 720912 | tf_op jit(solution)/shard_map/reduce_scatter | solution.py:311
  1249.4 60.0 %reduce-scatter.24.cloned.1.call-done = bf16[256,1408]{1,0:T(8,128)(2,1)} async-done(((bf16[2048,1408]{1,0:T(8,128)(2,1)}), bf16[256,1408]{1,0:T(8,128)(2,1)}) %reduce-scatter.24.cloned.1.call-update) | async-done | bytes 720912 | tf_op jit(solution)/shard_map/reduce_scatter | solution.py:314
  1311.8 59.9 %reduce-scatter.26.cloned.1.call-done = bf16[1408,256]{1,0:T(8,128)(2,1)} async-done(((bf16[1408,2048]{1,0:T(8,128)(2,1)}), bf16[1408,256]{1,0:T(8,128)(2,1)}) %reduce-scatter.26.cloned.1.call-update) | async-done | bytes 720912 | tf_op jit(solution)/shard_map/reduce_scatter | solution.py:317
  1374.0 52.6 %reduce-scatter.20.cloned.1.call-done = bf16[1024,256]{1,0:T(8,128)(2,1)} async-done(((bf16[1024,2048]{1,0:T(8,128)(2,1)}), bf16[1024,256]{1,0:T(8,128)(2,1)}) %reduce-scatter.20.cloned.1.call-update) | async-done | bytes 524304 | tf_op jit(solution)/shard_map/reduce_scatter | solution.py:305
  1444.7 23.3 %all-reduce.3 = (bf16[2048]{0:T(1024)(128)(2,1)S(1)}, bf16[1024]{0:T(1024)(128)(2,1)S(1)}, bf16[2048]{0:T(1024)(128)(2,1)S(1)}) all-reduce(bf16[2048]{0:T(1024)(128)(2,1)S(1)} %get-tuple-element.449, bf16[1024]{0:T(1024)(128)(2,1)} %get-tuple-element.451, ...), channel_id=3, replica_groups=mesh['fsdp'=4,'ctx'=2,'tp'=4] {'fsdp','ctx'}, use_global_device_ids=true, to_apply=%region_22.23.clone | all-reduce | flops 5120 | bytes 20480
  1469.9 17.0 %fusion.79 = (bf16[1,1024,2048]{2,1,0:T(8,128)(2,1)}, bf16[1,1024,2048]{2,1,0:T(8,128)(2,1)}) fusion(bf16[1,1024,2048]{2,1,0:T(8,128)(2,1)} %param.20, f32[1024,2048]{1,0:T(8,128)} %get-tuple-element.522, f32[1024]{0:T(1024)S(1)} %broadcast_multiply_fusion.1, f32[2048]{0:T(1024)S(1)} %bitcast.366, f32[1024]{0:T(1024)S(1)} %copy-done.36, ...), kind=kLoop, calls=%fused_computation.117 | loop fusion | flops 52428800 | bytes 37781504 | tf_op jit(solution)/shard_map/reshape | solution.py:285
  1488.4 17.0 %reduce-scatter.18.cloned.1.call-done = bf16[256,256]{1,0:T(8,128)(2,1)} async-done(((bf16[2048,256]{1,0:T(8,128)(2,1)}), bf16[256,256]{1,0:T(8,128)(2,1)}) %reduce-scatter.18.cloned.1.call-update) | async-done | bytes 131088 | tf_op jit(solution)/shard_map/reduce_scatter | solution.py:302
  1507.0 52.9 %reduce-scatter.12.cloned.1.call-done = bf16[256,1024]{1,0:T(8,128)(2,1)} async-done(((bf16[2048,1024]{1,0:T(8,128)(2,1)}), bf16[256,1024]{1,0:T(8,128)(2,1)}) %reduce-scatter.12.cloned.1.call-update) | async-done | bytes 524304 | tf_op jit(solution)/shard_map/reduce_scatter | solution.py:290
  (291 shorter events, 352.3 us)
Async XLA Ops:
  7.2 28.8 %all-gather.17.cloned.1.call-start = ((), (), s32[]{:S(2)}) async-start(), calls=%async_computation.11 | async-start | bytes 1179648 | tf_op jit(solution)/shard_map/all_gather | solution.py:108
  7.9 53.4 %all-gather.19.cloned.1.call-start = ((), (), s32[]{:S(2)}) async-start(), calls=%async_computation.12 | async-start | bytes 1179648 | tf_op jit(solution)/shard_map/all_gather | solution.py:109
  8.7 71.0 %all-gather.21.cloned.1.call-start = ((), (), s32[]{:S(2)}) async-start(), calls=%async_computation.13 | async-start | bytes 3145728 | tf_op jit(solution)/shard_map/all_gather | solution.py:145
  19.8 96.9 %copy-start.25 = (f32[8,1,256]{2,1,0:T(1,128)}, f32[8,1,256]{2,1,0:T(1,128)S(1)}, u32[]{:S(2)}) copy-start(f32[8,1,256]{2,1,0:T(1,128)S(1)} %convert_element_type.302) | copy-start | bytes 24580
  23.0 93.7 %copy-start.35 = (f32[1024]{0:T(1024)}, f32[1024]{0:T(1024)S(1)}, u32[]{:S(2)}) copy-start(f32[1024]{0:T(1024)S(1)} %add_rsqrt_fusion.2) | copy-start | bytes 12292
  66.4 50.3 %all-gather.13.cloned.1.call-start = ((), (), s32[]{:S(2)}) async-start(), calls=%async_computation.9 | async-start | bytes 4718592 | tf_op jit(solution)/shard_map/all_gather | solution.py:105
  67.0 79.2 %all-gather.15.cloned.1.call-start = ((), (), s32[]{:S(2)}) async-start(), calls=%async_computation.10 | async-start | bytes 2359296 | tf_op jit(solution)/shard_map/all_gather | solution.py:107
  67.5 139.4 %all-gather.23.cloned.1.call-start = ((), (), s32[]{:S(2)}) async-start(), calls=%async_computation.14 | async-start | bytes 4718592 | tf_op jit(solution)/shard_map/all_gather | solution.py:110
  68.1 303.3 %all-reduce.9.cloned.1.call-start = ((), (), s32[]{:S(2)}) async-start(), calls=%async_computation.15 | async-start | bytes 8388608 | tf_op jit(solution)/shard_map/psum | solution.py:186
  70.1 89.7 %copy-start.14 = (f32[1024,128]{1,0:T(8,128)}, f32[1024,128]{1,0:T(8,128)S(1)}, u32[]{:S(2)}) copy-start(f32[1024,128]{1,0:T(8,128)S(1)} %get-tuple-element.518) | copy-start | bytes 1572868
  70.1 89.7 %copy-start.16 = (f32[1024,128]{1,0:T(8,128)}, f32[1024,128]{1,0:T(8,128)S(1)}, u32[]{:S(2)}) copy-start(f32[1024,128]{1,0:T(8,128)S(1)} %get-tuple-element.519) | copy-start | bytes 1572868
  216.3 199.2 %all-gather.25.cloned.1.call-start = ((), (), s32[]{:S(2)}) async-start(), calls=%async_computation.16 | async-start | bytes 6488064 | tf_op jit(solution)/shard_map/all_gather | solution.py:112
  217.1 243.5 %all-gather.27.cloned.1.call-start = ((), (), s32[]{:S(2)}) async-start(), calls=%async_computation.17 | async-start | bytes 6488064 | tf_op jit(solution)/shard_map/all_gather | solution.py:113
  217.8 288.8 %all-gather.29.cloned.1.call-start = ((), (), s32[]{:S(2)}) async-start(), calls=%async_computation.18 | async-start | bytes 6488064 | tf_op jit(solution)/shard_map/all_gather | solution.py:114
  218.4 478.6 %all-reduce.11.cloned.1.call-start = ((), (), s32[]{:S(2)}) async-start(), calls=%async_computation.19 | async-start | bytes 8388608 | tf_op jit(solution)/shard_map/psum | solution.py:209
  227.4 477.9 %copy-start.23 = (f32[8,1,256]{2,1,0:T(1,128)}, f32[8,1,256]{2,1,0:T(1,128)S(1)}, u32[]{:S(2)}) copy-start(f32[8,1,256]{2,1,0:T(1,128)S(1)} %convert_element_type.304) | copy-start | bytes 24580
  376.5 328.8 %copy-start.29 = (f32[1024]{0:T(1024)}, f32[1024]{0:T(1024)S(1)}, u32[]{:S(2)}) copy-start(f32[1024]{0:T(1024)S(1)} %add_rsqrt_fusion) | copy-start | bytes 12292
  541.9 343.7 %reduce-scatter.10.cloned.1.call-start = ((), (), s32[]{:S(2)}) async-start(), calls=%async_computation.20 | async-start | bytes 3145728 | tf_op jit(solution)/shard_map/reduce_scatter | solution.py:261
  863.2 278.4 %all-reduce.13.cloned.1.call-start = ((), (), s32[]{:S(2)}) async-start(), calls=%async_computation.29 | async-start | bytes 14680064 | tf_op jit(solution)/shard_map/psum | solution.py:196
  885.7 299.1 %reduce-scatter.14.cloned.1.call-start = ((), (), s32[]{:S(2)}) async-start(), calls=%async_computation.22 | async-start | bytes 2359296 | tf_op jit(solution)/shard_map/reduce_scatter | solution.py:296
  893.1 354.0 %reduce-scatter.22.cloned.1.call-start = ((), (), s32[]{:S(2)}) async-start(), calls=%async_computation.26 | async-start | bytes 6488064 | tf_op jit(solution)/shard_map/reduce_scatter | solution.py:311
  904.2 405.2 %reduce-scatter.24.cloned.1.call-start = ((), (), s32[]{:S(2)}) async-start(), calls=%async_computation.27 | async-start | bytes 6488064 | tf_op jit(solution)/shard_map/reduce_scatter | solution.py:314
  915.4 456.3 %reduce-scatter.26.cloned.1.call-start = ((), (), s32[]{:S(2)}) async-start(), calls=%async_computation.28 | async-start | bytes 6488064 | tf_op jit(solution)/shard_map/reduce_scatter | solution.py:317
  926.0 500.6 %reduce-scatter.20.cloned.1.call-start = ((), (), s32[]{:S(2)}) async-start(), calls=%async_computation.25 | async-start | bytes 4718592 | tf_op jit(solution)/shard_map/reduce_scatter | solution.py:305
  942.3 200.9 %copy-start.28 = (f32[1024]{0:T(1024)S(1)}, f32[1024]{0:T(1024)}, u32[]{:S(2)}) copy-start(f32[1024]{0:T(1024)} %copy-done.27) | copy-start | bytes 12292
  942.3 201.0 %copy-start.41 = (f32[128]{0:T(128)S(1)}, f32[128]{0:T(128)}, u32[]{:S(2)}) copy-start(f32[128]{0:T(128)} %copy-done.40) | copy-start | bytes 1540
  942.3 203.3 %copy-start.26 = (f32[8,1,256]{2,1,0:T(1,128)S(1)}, f32[8,1,256]{2,1,0:T(1,128)}, u32[]{:S(2)}) copy-start(f32[8,1,256]{2,1,0:T(1,128)} %copy-done.25) | copy-start | bytes 24580
  942.3 203.3 %copy-start.36 = (f32[1024]{0:T(1024)S(1)}, f32[1024]{0:T(1024)}, u32[]{:S(2)}) copy-start(f32[1024]{0:T(1024)} %copy-done.35) | copy-start | bytes 12292
  942.3 544.5 %reduce-scatter.16.cloned.1.call-start = ((), (), s32[]{:S(2)}) async-start(), calls=%async_computation.23 | async-start | bytes 1179648 | tf_op jit(solution)/shard_map/reduce_scatter | solution.py:299
  1148.4 357.0 %reduce-scatter.18.cloned.1.call-start = ((), (), s32[]{:S(2)}) async-start(), calls=%async_computation.24 | async-start | bytes 1179648 | tf_op jit(solution)/shard_map/reduce_scatter | solution.py:302
  1155.7 404.3 %reduce-scatter.12.cloned.1.call-start = ((), (), s32[]{:S(2)}) async-start(), calls=%async_computation.21 | async-start | bytes 4718592 | tf_op jit(solution)/shard_map/reduce_scatter | solution.py:290
  1186.6 242.0 %copy-start.22 = (bf16[2048,256]{1,0:T(8,128)(2,1)S(1)}, bf16[2048,256]{1,0:T(8,128)(2,1)}, u32[]{:S(2)}) copy-start(bf16[2048,256]{1,0:T(8,128)(2,1)} %all-gather.17.cloned.1.call-done) | copy-start | bytes 3145732
  (50 other events, 573.0 us)
Sparse Core Ops, SparseCore 0:
  9.9 26.0 all-gather.16
  37.9 23.3 all-gather.18
  66.5 10.5 all-gather.20
  78.8 37.7 all-gather.12
  118.4 27.7 all-gather.14
  147.9 37.3 all-gather.22
  216.5 154.9 all-reduce.8
  373.3 42.1 all-gather.24
  417.4 43.1 all-gather.26
  462.4 44.2 all-gather.28
  542.0 154.9 all-reduce.10
  863.3 8.5 reduce-scatter.9
  885.8 255.7 all-reduce.12
  1144.8 39.9 reduce-scatter.13
  1188.1 58.9 reduce-scatter.21
  1250.4 58.9 reduce-scatter.23
  1312.7 58.8 reduce-scatter.25
  1375.5 51.0 reduce-scatter.19
  1430.3 36.1 reduce-scatter.15
  1469.5 35.8 reduce-scatter.17
  1508.8 51.1 reduce-scatter.11
where the time goes:
time: 1580 us; the launch traced here: 1570 us
  waiting for transfers between devices  1010 us (64%)
  matrix products  303 us (19%)
  other arithmetic  146 us (9%)
  blocking collectives  51.8 us (3%)
  local copies, waits for them, and re-layouts  30.2 us (2%)
  between operations  16.7 us (1%)
    psum x1, waiting for transfers between devices, shards(): lax.psum(ffn_terms.astype(jnp.bfloat16), 'tp').astype(jnp.float32)  199 us
    psum x1, waiting for transfers between devices, shards(): lax.psum(d_norm_terms.astype(jnp.bfloat16), 'tp').astype(jnp.float32)  155 us
    psum x1, waiting for transfers between devices, shards(): lax.psum(attn_terms.astype(jnp.bfloat16), 'tp').astype(jnp.float32)  144 us
    dot_general x8, matrix products, matmul(): return jnp.dot(left, right, preferred_element_type=jnp.float32)  67.2 us
    dot_general x8, matrix products, matmul_tn(): lax.dot_general(left, right, (((0,), (0,)), ((), ())), preferred_element_...  66.1 us
    dot_general x8, matrix products, matmul_nt(): lax.dot_general(left, right, (((1,), (1,)), ((), ())), preferred_element_...  65.2 us
    reduce_scatter x1, waiting for transfers between devices, shards(): lax.psum_scatter(gate_grad.astype(jnp.bfloat16), ('fsdp', 'ctx'), scatter...  60.5 us
    reduce_scatter x1, waiting for transfers between devices, shards(): lax.psum_scatter(up_grad.astype(jnp.bfloat16), ('fsdp', 'ctx'), scatter_d...  60 us
  transfers between devices with their start and end apart: 21, of which 17 were waited for; matrix products, arithmetic and copies ran while one was open for 17% of the time, Pallas kernels for 0%

commit v1 on v0

--- a/solution.py
+++ b/solution.py
@@ -206,7 +206,9 @@
     gate_grad = matmul_tn(normed_two, d_gate)
     up_grad = matmul_tn(normed_two, d_up)
     d_norm_terms = matmul_nt(d_gate, full_gate_proj) + matmul_nt(d_up, full_up_proj)
-    d_normed_two = lax.psum(d_norm_terms.astype(jnp.bfloat16), "tp").astype(jnp.float32)
+    d_normed_two = jnp.sum(lax.all_gather(d_norm_terms.astype(jnp.bfloat16), "tp"), axis=0).astype(
+        jnp.float32
+    )
     d_hidden_norm, ffn_gain_grad = norm_back(hidden_part, inverse_two, full_ffn_gain, d_normed_two)
     d_hidden = upstream.astype(jnp.float32) + d_hidden_norm
     d_mixed = d_hidden.astype(jnp.bfloat16)

time: 1580 us -> 1720 us (1.089)
  waiting for transfers between devices: 1010 us -> 1130 us
    all_gather x0 -> x1, waiting for transfers between devices: none -> 287 us  [shards(): lax.all_gather(d_norm_terms.astype(jnp.bfloat16), 'tp')]
    psum x1 -> x0, waiting for transfers between devices: 155 us -> none  [shards(): lax.psum(d_norm_terms.astype(jnp.bfloat16), 'tp').astype(jnp.float32)]
    reduce_scatter x1, waiting for transfers between devices: 60.5 us -> 31.1 us  [shards(): lax.psum_scatter(gate_grad.astype(jnp.bfloat16), ('fsdp', 'ctx'), scatter...]
    reduce_scatter x1, waiting for transfers between devices: 13.9 us -> 42 us  [shards(): lax.psum_scatter(query_up_grad.astype(jnp.bfloat16), ('fsdp', 'ctx'), sca...]
  transfers between devices with their start and end apart: 21 -> 21, of which waited for: 17 -> 17; matrix products, arithmetic and copies ran while one was open for 17% -> 15% of each run, Pallas kernels for 0% -> 0%
where the time goes in v1:
time: 1720 us; the launch traced here: 1710 us
  waiting for transfers between devices  1130 us (66%)
  matrix products  304 us (18%)
  other arithmetic  159 us (9%)
  blocking collectives  51.4 us (3%)
  local copies, waits for them, and re-layouts  33.9 us (2%)
    all_gather x1, waiting for transfers between devices, shards(): lax.all_gather(d_norm_terms.astype(jnp.bfloat16), 'tp')  287 us
    psum x1, waiting for transfers between devices, shards(): lax.psum(ffn_terms.astype(jnp.bfloat16), 'tp').astype(jnp.float32)  194 us
    psum x1, waiting for transfers between devices, shards(): lax.psum(attn_terms.astype(jnp.bfloat16), 'tp').astype(jnp.float32)  144 us
    dot_general x8, matrix products, matmul(): return jnp.dot(left, right, preferred_element_type=jnp.float32)  67.2 us
    dot_general x8, matrix products, matmul_tn(): lax.dot_general(left, right, (((0,), (0,)), ((), ())), preferred_element_...  67 us
    dot_general x8, matrix products, matmul_nt(): lax.dot_general(left, right, (((1,), (1,)), ((), ())), preferred_element_...  65.2 us
    reduce_scatter x1, waiting for transfers between devices, shards(): lax.psum_scatter(up_grad.astype(jnp.bfloat16), ('fsdp', 'ctx'), scatter_d...  60 us
    reduce_scatter x1, waiting for transfers between devices, shards(): lax.psum_scatter(down_grad.astype(jnp.bfloat16), ('fsdp', 'ctx'), scatter...  59.9 us
  transfers between devices with their start and end apart: 21, of which 17 were waited for; matrix products, arithmetic and copies ran while one was open for 15% of the time, Pallas kernels for 0%

profile of v1, /device:TPU:0, one launch (start us, length us, event | category | flops | bytes accessed | tf_op | source)
XLA Modules:
  0.0 1713.2 jit_solution(1526639759532501683)
XLA Ops:
  23.0 13.0 all-gather.19.cloned.1.call-done
  42.3 19.0 %all-gather.21.cloned.1.call-done = bf16[2048,256]{1,0:T(8,128)(2,1)} async-done(((bf16[256,256]{1,0:T(8,128)(2,1)}), bf16[2048,256]{1,0:T(8,128)(2,1)}) %all-gather.21.cloned.1.call-update) | async-done | bytes 1048592 | tf_op jit(solution)/shard_map/all_gather | solution.py:109
  82.2 34.4 %all-gather.15.cloned.1.call-done = bf16[2048,1024]{1,0:T(8,128)(2,1)} async-done(((bf16[256,1024]{1,0:T(8,128)(2,1)}), bf16[2048,1024]{1,0:T(8,128)(2,1)}) %all-gather.15.cloned.1.call-update) | async-done | bytes 4194320 | tf_op jit(solution)/shard_map/all_gather | solution.py:105
  126.8 19.4 %all-gather.17.cloned.1.call-done = bf16[1024,1024]{1,0:T(8,128)(2,1)} async-done(((bf16[128,1024]{1,0:T(8,128)(2,1)}), bf16[1024,1024]{1,0:T(8,128)(2,1)}) %all-gather.17.cloned.1.call-update) | async-done | bytes 2097168 | tf_op jit(solution)/shard_map/all_gather | solution.py:107
  164.1 38.1 %while.31 = (s32[]{:T(128)}, bf16[2,512,4,256]{3,1,2,0:T(8,128)(2,1)}, f32[2,4,512]{2,1,0:T(4,128)S(1)}, s32[2]{0:T(128)S(1)}, s32[1024]{0:T(1024)S(1)}, /*index...) while((s32[]{:T(128)}, ...), condition=%wide.region_6.7_spmd.clone, body=%wide.region_3.6_spmd.clone.sunk | while | flops 4349491712 | bytes 59858748 | solution.py:183
  227.8 144.1 %all-reduce.8.cloned.1.call-done = bf16[1024,2048]{1,0:T(8,128)(2,1)} async-done(((bf16[1024,2048]{1,0:T(8,128)(2,1)}), bf16[1024,2048]{1,0:T(8,128)(2,1)}) %all-reduce.8.cloned.1.call-update) | async-done | bytes 4194320 | tf_op jit(solution)/shard_map/psum | solution.py:186
  382.0 34.0 %all-gather.27.cloned.1.call-done = bf16[2048,1408]{1,0:T(8,128)(2,1)} async-done(((bf16[256,1408]{1,0:T(8,128)(2,1)}), bf16[2048,1408]{1,0:T(8,128)(2,1)}) %all-gather.27.cloned.1.call-update) | async-done | bytes 5767184 | tf_op jit(solution)/shard_map/all_gather | solution.py:112
  415.9 11.7 fusion.130
  427.6 33.5 %all-gather.29.cloned.1.call-done = bf16[2048,1408]{1,0:T(8,128)(2,1)} async-done(((bf16[256,1408]{1,0:T(8,128)(2,1)}), bf16[2048,1408]{1,0:T(8,128)(2,1)}) %all-gather.29.cloned.1.call-update) | async-done | bytes 5767184 | tf_op jit(solution)/shard_map/all_gather | solution.py:113
  461.0 11.7 fusion.131
  472.7 34.3 %all-gather.31.cloned.1.call-done = bf16[1408,2048]{1,0:T(8,128)(2,1)} async-done(((bf16[1408,256]{1,0:T(8,128)(2,1)}), bf16[1408,2048]{1,0:T(8,128)(2,1)}) %all-gather.31.cloned.1.call-update) | async-done | bytes 5767184 | tf_op jit(solution)/shard_map/all_gather | solution.py:114
  507.1 15.6 multiply_convert_fusion.1
  542.4 286.8 %all-gather.33.cloned.1.call-done = bf16[4096,2048]{1,0:T(8,128)(2,1)} async-done(((bf16[1024,2048]{1,0:T(8,128)(2,1)}), bf16[4096,2048]{1,0:T(8,128)(2,1)}) %all-gather.33.cloned.1.call-update) | async-done | bytes 16777232 | tf_op jit(solution)/shard_map/all_gather | solution.py:209
  829.2 12.1 reduce_sum.130
  859.3 144.5 %while.32 = (s32[]{:T(128)}, f32[1,2048,512]{1,2,0:T(8,128)}, f32[2,512,4,256]{3,1,0,2:T(8,128)}, s32[2]{0:T(128)S(1)}, s32[1024]{0:T(1024)S(1)}, /*index=5*/s32...) while((s32[]{:T(128)}, f32[1,2048,512]{1,2,0:T(8,128)}, ...), condition=%wide.region_15.16_spmd.clone, body=%wide.region_12.15_spmd.clone.sunk | while | flops 10809767936 | bytes 248594592 | solution.py:250
  874.2 13.2 fusion.193
  887.5 15.9 fusion.194
  945.6 13.2 fusion.193
  958.8 15.9 fusion.194
  1007.9 11.0 convolution_convert_fusion.3
  1032.1 11.2 convolution_convert_fusion.2
  1076.1 14.8 convolution_convert_fusion.4
  1091.0 194.5 %all-reduce.10.cloned.1.call-done = (bf16[1024,2048]{1,0:T(8,128)(2,1)}, bf16[1024,1024]{0,1:T(8,128)(2,1)}, bf16[1,1024,512]{1,2,0:T(8,128)(2,1)}) async-done(((bf16[1024,2048]{1,0:T(8,128)(2,1)}, bf16[1024,1024]{0,1:T(8,128)(2,1)}, bf16[1,1024,512]{1,2,0:T(8,128)(2,1)}), (bf16[1024,2048]{1,0:T(8,128)(2,1)}, bf16[1024,1024]{0,1:T(8,128)(2,1)}, ...) | async-done | bytes 7340048 | tf_op jit(solution)/shard_map/psum | solution.py:196
  1315.6 31.1 %reduce-scatter.22.cloned.1.call-done = bf16[256,1408]{1,0:T(8,128)(2,1)} async-done(((bf16[2048,1408]{1,0:T(8,128)(2,1)}), bf16[256,1408]{1,0:T(8,128)(2,1)}) %reduce-scatter.22.cloned.1.call-update) | async-done | bytes 720912 | tf_op jit(solution)/shard_map/reduce_scatter | solution.py:313
  1349.0 60.0 %reduce-scatter.24.cloned.1.call-done = bf16[256,1408]{1,0:T(8,128)(2,1)} async-done(((bf16[2048,1408]{1,0:T(8,128)(2,1)}), bf16[256,1408]{1,0:T(8,128)(2,1)}) %reduce-scatter.24.cloned.1.call-update) | async-done | bytes 720912 | tf_op jit(solution)/shard_map/reduce_scatter | solution.py:316
  1411.3 59.9 %reduce-scatter.26.cloned.1.call-done = bf16[1408,256]{1,0:T(8,128)(2,1)} async-done(((bf16[1408,2048]{1,0:T(8,128)(2,1)}), bf16[1408,256]{1,0:T(8,128)(2,1)}) %reduce-scatter.26.cloned.1.call-update) | async-done | bytes 720912 | tf_op jit(solution)/shard_map/reduce_scatter | solution.py:319
  1473.5 42.0 %reduce-scatter.14.cloned.1.call-done = bf16[128,1024]{1,0:T(8,128)(2,1)} async-done(((bf16[1024,1024]{1,0:T(8,128)(2,1)}), bf16[128,1024]{1,0:T(8,128)(2,1)}) %reduce-scatter.14.cloned.1.call-update) | async-done | bytes 262160 | tf_op jit(solution)/shard_map/reduce_scatter | solution.py:298
  1517.3 53.1 %reduce-scatter.20.cloned.1.call-done = bf16[1024,256]{1,0:T(8,128)(2,1)} async-done(((bf16[1024,2048]{1,0:T(8,128)(2,1)}), bf16[1024,256]{1,0:T(8,128)(2,1)}) %reduce-scatter.20.cloned.1.call-update) | async-done | bytes 524304 | tf_op jit(solution)/shard_map/reduce_scatter | solution.py:307
  1588.6 23.3 %all-reduce.3 = (bf16[2048]{0:T(1024)(128)(2,1)S(1)}, bf16[1024]{0:T(1024)(128)(2,1)S(1)}, bf16[2048]{0:T(1024)(128)(2,1)S(1)}) all-reduce(bf16[2048]{0:T(1024)(128)(2,1)S(1)} %get-tuple-element.449, bf16[1024]{0:T(1024)(128)(2,1)} %get-tuple-element.451, ...), channel_id=4, replica_groups=mesh['fsdp'=4,'ctx'=2,'tp'=4] {'fsdp','ctx'}, use_global_device_ids=true, to_apply=%region_22.23.clone | all-reduce | flops 5120 | bytes 20480
  1613.7 17.0 fusion.79
  1632.3 17.0 reduce-scatter.18.cloned.1.call-done
  1650.9 52.9 %reduce-scatter.12.cloned.1.call-done = bf16[256,1024]{1,0:T(8,128)(2,1)} async-done(((bf16[2048,1024]{1,0:T(8,128)(2,1)}), bf16[256,1024]{1,0:T(8,128)(2,1)}) %reduce-scatter.12.cloned.1.call-update) | async-done | bytes 524304 | tf_op jit(solution)/shard_map/reduce_scatter | solution.py:292
  (296 shorter events, 367.9 us)
Async XLA Ops:
  7.2 28.8 %all-gather.19.cloned.1.call-start = ((), (), s32[]{:S(2)}) async-start(), calls=%async_computation.11 | async-start | bytes 1179648 | tf_op jit(solution)/shard_map/all_gather | solution.py:108
  7.9 53.4 %all-gather.21.cloned.1.call-start = ((), (), s32[]{:S(2)}) async-start(), calls=%async_computation.12 | async-start | bytes 1179648 | tf_op jit(solution)/shard_map/all_gather | solution.py:109
  8.7 70.7 %all-gather.23.cloned.1.call-start = ((), (), s32[]{:S(2)}) async-start(), calls=%async_computation.13 | async-start | bytes 3145728 | tf_op jit(solution)/shard_map/all_gather | solution.py:145
  19.8 96.9 %copy-start.24 = (f32[8,1,256]{2,1,0:T(1,128)}, f32[8,1,256]{2,1,0:T(1,128)S(1)}, u32[]{:S(2)}) copy-start(f32[8,1,256]{2,1,0:T(1,128)S(1)} %convert_element_type.304) | copy-start | bytes 24580
  23.0 93.7 %copy-start.34 = (f32[1024]{0:T(1024)}, f32[1024]{0:T(1024)S(1)}, u32[]{:S(2)}) copy-start(f32[1024]{0:T(1024)S(1)} %add_rsqrt_fusion.2) | copy-start | bytes 12292
  66.4 50.3 %all-gather.15.cloned.1.call-start = ((), (), s32[]{:S(2)}) async-start(), calls=%async_computation.9 | async-start | bytes 4718592 | tf_op jit(solution)/shard_map/all_gather | solution.py:105
  67.0 79.2 %all-gather.17.cloned.1.call-start = ((), (), s32[]{:S(2)}) async-start(), calls=%async_computation.10 | async-start | bytes 2359296 | tf_op jit(solution)/shard_map/all_gather | solution.py:107
  67.5 139.9 %all-gather.25.cloned.1.call-start = ((), (), s32[]{:S(2)}) async-start(), calls=%async_computation.14 | async-start | bytes 4718592 | tf_op jit(solution)/shard_map/all_gather | solution.py:110
  68.1 303.7 %all-reduce.8.cloned.1.call-start = ((), (), s32[]{:S(2)}) async-start(), calls=%async_computation.15 | async-start | bytes 8388608 | tf_op jit(solution)/shard_map/psum | solution.py:186
  70.1 89.7 %copy-start.14 = (f32[1024,128]{1,0:T(8,128)}, f32[1024,128]{1,0:T(8,128)S(1)}, u32[]{:S(2)}) copy-start(f32[1024,128]{1,0:T(8,128)S(1)} %get-tuple-element.518) | copy-start | bytes 1572868
  70.1 89.7 %copy-start.16 = (f32[1024,128]{1,0:T(8,128)}, f32[1024,128]{1,0:T(8,128)S(1)}, u32[]{:S(2)}) copy-start(f32[1024,128]{1,0:T(8,128)S(1)} %get-tuple-element.519) | copy-start | bytes 1572868
  216.8 199.1 %all-gather.27.cloned.1.call-start = ((), (), s32[]{:S(2)}) async-start(), calls=%async_computation.16 | async-start | bytes 6488064 | tf_op jit(solution)/shard_map/all_gather | solution.py:112
  217.6 243.5 %all-gather.29.cloned.1.call-start = ((), (), s32[]{:S(2)}) async-start(), calls=%async_computation.17 | async-start | bytes 6488064 | tf_op jit(solution)/shard_map/all_gather | solution.py:113
  218.3 288.8 %all-gather.31.cloned.1.call-start = ((), (), s32[]{:S(2)}) async-start(), calls=%async_computation.18 | async-start | bytes 6488064 | tf_op jit(solution)/shard_map/all_gather | solution.py:114
  218.9 610.3 %all-gather.33.cloned.1.call-start = ((), (), s32[]{:S(2)}) async-start(), calls=%async_computation.28 | async-start | bytes 20971520 | tf_op jit(solution)/shard_map/all_gather | solution.py:209
  227.8 621.8 %copy-start.22 = (f32[8,1,256]{2,1,0:T(1,128)}, f32[8,1,256]{2,1,0:T(1,128)S(1)}, u32[]{:S(2)}) copy-start(f32[8,1,256]{2,1,0:T(1,128)S(1)} %convert_element_type.306) | copy-start | bytes 24580
  376.9 472.7 %copy-start.28 = (f32[1024]{0:T(1024)}, f32[1024]{0:T(1024)S(1)}, u32[]{:S(2)}) copy-start(f32[1024]{0:T(1024)S(1)} %add_rsqrt_fusion) | copy-start | bytes 12292
  542.3 488.0 %reduce-scatter.10.cloned.1.call-start = ((), (), s32[]{:S(2)}) async-start(), calls=%async_computation.19 | async-start | bytes 3145728 | tf_op jit(solution)/shard_map/reduce_scatter | solution.py:263
  1007.8 277.7 %all-reduce.10.cloned.1.call-start = ((), (), s32[]{:S(2)}) async-start(), calls=%async_computation.29 | async-start | bytes 14680064 | tf_op jit(solution)/shard_map/psum | solution.py:196
  1030.3 316.4 %reduce-scatter.22.cloned.1.call-start = ((), (), s32[]{:S(2)}) async-start(), calls=%async_computation.25 | async-start | bytes 6488064 | tf_op jit(solution)/shard_map/reduce_scatter | solution.py:313
  1043.3 365.7 %reduce-scatter.24.cloned.1.call-start = ((), (), s32[]{:S(2)}) async-start(), calls=%async_computation.26 | async-start | bytes 6488064 | tf_op jit(solution)/shard_map/reduce_scatter | solution.py:316
  1055.9 415.3 %reduce-scatter.26.cloned.1.call-start = ((), (), s32[]{:S(2)}) async-start(), calls=%async_computation.27 | async-start | bytes 6488064 | tf_op jit(solution)/shard_map/reduce_scatter | solution.py:319
  1068.6 446.9 %reduce-scatter.14.cloned.1.call-start = ((), (), s32[]{:S(2)}) async-start(), calls=%async_computation.21 | async-start | bytes 2359296 | tf_op jit(solution)/shard_map/reduce_scatter | solution.py:298
  1075.9 494.6 %reduce-scatter.20.cloned.1.call-start = ((), (), s32[]{:S(2)}) async-start(), calls=%async_computation.24 | async-start | bytes 4718592 | tf_op jit(solution)/shard_map/reduce_scatter | solution.py:307
  1090.9 196.2 %copy-start.27 = (f32[1024]{0:T(1024)S(1)}, f32[1024]{0:T(1024)}, u32[]{:S(2)}) copy-start(f32[1024]{0:T(1024)} %copy-done.26) | copy-start | bytes 12292
  1090.9 196.2 %copy-start.40 = (f32[128]{0:T(128)S(1)}, f32[128]{0:T(128)}, u32[]{:S(2)}) copy-start(f32[128]{0:T(128)} %copy-done.39) | copy-start | bytes 1540
  1090.9 198.5 %copy-start.25 = (f32[8,1,256]{2,1,0:T(1,128)S(1)}, f32[8,1,256]{2,1,0:T(1,128)}, u32[]{:S(2)}) copy-start(f32[8,1,256]{2,1,0:T(1,128)} %copy-done.24) | copy-start | bytes 24580
  1090.9 198.5 %copy-start.35 = (f32[1024]{0:T(1024)S(1)}, f32[1024]{0:T(1024)}, u32[]{:S(2)}) copy-start(f32[1024]{0:T(1024)} %copy-done.34) | copy-start | bytes 12292
  1091.0 539.7 %reduce-scatter.16.cloned.1.call-start = ((), (), s32[]{:S(2)}) async-start(), calls=%async_computation.22 | async-start | bytes 1179648 | tf_op jit(solution)/shard_map/reduce_scatter | solution.py:301
  1292.3 357.0 %reduce-scatter.18.cloned.1.call-start = ((), (), s32[]{:S(2)}) async-start(), calls=%async_computation.23 | async-start | bytes 1179648 | tf_op jit(solution)/shard_map/reduce_scatter | solution.py:304
  1300.2 403.6 %reduce-scatter.12.cloned.1.call-start = ((), (), s32[]{:S(2)}) async-start(), calls=%async_computation.20 | async-start | bytes 4718592 | tf_op jit(solution)/shard_map/reduce_scatter | solution.py:292
  1315.6 256.9 %copy-start.21 = (bf16[2048,256]{1,0:T(8,128)(2,1)S(1)}, bf16[2048,256]{1,0:T(8,128)(2,1)}, u32[]{:S(2)}) copy-start(bf16[2048,256]{1,0:T(8,128)(2,1)} %all-gather.19.cloned.1.call-done) | copy-start | bytes 3145732
  (52 other events, 600.0 us)
Sparse Core Ops, SparseCore 0:
  9.9 26.0 all-gather.18
  37.9 23.3 all-gather.20
  66.5 10.5 all-gather.22
  78.8 37.7 all-gather.14
  118.4 27.7 all-gather.16
  147.9 37.3 all-gather.24
  216.9 154.8 all-reduce.7
  373.7 42.1 all-gather.26
  417.8 43.1 all-gather.28
  462.8 44.2 all-gather.30
  542.4 286.7 all-gather.32
  1007.9 7.7 reduce-scatter.9
  1030.4 254.9 all-reduce.9
  1288.8 57.8 reduce-scatter.21
  1350.0 59.0 reduce-scatter.23
  1412.3 58.8 reduce-scatter.25
  1474.4 41.1 reduce-scatter.13
  1519.3 51.0 reduce-scatter.19
  1574.2 36.1 reduce-scatter.15
  1613.4 35.8 reduce-scatter.17
  1652.6 51.1 reduce-scatter.11
